TPU v7x, 128 devices: a whole 4x4x4 slice. The times are simulated.
128 devices in a mesh: patch: 2 (over core), cells: 64 (over y, x, z).
Axes of the slice: x: 4, y: 4, z: 4, core: 2. Of those that a mesh axis runs over, the one named last changes fastest.
Arguments:
- features: bfloat16 [128, 1024, 512], P('cells', 'patch'), may hold values from -6 to 6
- hilbert_rank: int32 [128, 32], P('cells', 'patch'), may hold values from 0 to 4095, as said below
- valid_count: int32 [128, 32], P('cells', 'patch'), may hold values from 1 to 32
- norm_gains: float32 [3, 512], replicated
- w_qkv: bfloat16 [512, 1536], replicated
- w_out: bfloat16 [512, 512], replicated, may hold values from -0.25 to 0.25
- w_up: bfloat16 [2, 512, 2048], replicated, may hold values from -0.25 to 0.25
- w_down: bfloat16 [2, 2048, 512], replicated, may hold values from -0.125 to 0.125
Outputs:
- final: bfloat16 [128, 1024, 512], P('cells', 'patch')
Inputs may be any that keep to these rules, and one draw needn't show every extreme that they name: `hilbert_rank`: a permutation of all cells; a cell keeps its half of a patch (its index within the patch divided by 16 stays the same); the 32 cells of one device go to exactly 32 owners along cells (the device itself may be one), 1 cells to each.
All inputs are finite; a program needn't handle non-finite values.
Results may differ from a plain program's by a relative error of at most 0.013.
The roundings to bfloat16 on the way count: a program that leaves them out, or rounds other values in their place, can miss the bound.
Values may be sent and summed in bfloat16 or wider, within the bound.
A program may use at most 128 MiB of HBM per device.

v0:
```python
import functools
import itertools
import math
import random

import jax
import jax.numpy as jnp
from jax import lax
from jax.experimental import pallas as pl
from jax.experimental.pallas import tpu as pltpu
from jax.sharding import PartitionSpec as P

MESH = pl.DeviceIdType.MESH
EPSILON = 1e-05
C = 512
FF = 2048
CELL = 32
SIDE = 4
SLOTS = SIDE**3
CELLS_DEV = 32
HALF_CELLS = 16
HALF_ROWS = 512
PATCH_ROWS = 1024
GROUPS = 4
GROUP_LANES = 128
GROUP_HEADS = 8
DEPTH = 16
GELU_LINEAR = math.sqrt(2 / math.pi)
GELU_CUBIC = 0.044715 * GELU_LINEAR
QUERY_SCALE = DEPTH**-0.5 * math.log2(math.e)
TM = 128
TQ = 32
TK = 128
STACK = GROUP_HEADS * TQ
FORWARD_LIMIT = 48 * 1024 * 1024
LAYER_LIMIT = 32 * 1024 * 1024
RETURN_LIMIT = 20 * 1024 * 1024

OFFSETS = [o for o in itertools.product(range(SIDE), repeat=3) if o != (0, 0, 0)]
random.Random(0).shuffle(OFFSETS)
OFFSETS = [(0, 0, 0)] + OFFSETS
BATCH = 4
BATCHES = SLOTS // BATCH


def number(offset):
    return (offset[0] * SIDE + offset[1]) * SIDE + offset[2]


def peers(sign):
    me = lax.axis_index("cells")
    ys = [lax.rem(lax.div(me, 16) + d, SIDE) * 16 for d in range(SIDE)]
    xs = [lax.rem(lax.div(me, 4) + d, SIDE) * 4 for d in range(SIDE)]
    zs = [lax.rem(me + d, SIDE) for d in range(SIDE)]
    return [
        ys[sign * oy % SIDE] + xs[sign * ox % SIDE] + zs[sign * oz % SIDE]
        for oy, ox, oz in OFFSETS
    ]


def norm_rows(values, gains):
    center = values - jnp.mean(values, axis=-1, keepdims=True)
    spread = jnp.mean(center * center, axis=-1, keepdims=True)
    return (center * lax.rsqrt(spread + EPSILON) * gains).astype(jnp.bfloat16)


def gelu(value):
    inner = value * (GELU_LINEAR + GELU_CUBIC * (value * value))
    half = 0.5 * value
    return (half + half * jnp.tanh(inner)).astype(jnp.bfloat16)


def mlp_rows(rows, gain_row, w_up, w_down):
    normed = norm_rows(rows, gain_row)
    raised = jnp.dot(normed, w_up[...], preferred_element_type=jnp.float32)
    return rows + jnp.dot(gelu(raised), w_down[...], preferred_element_type=jnp.float32)


def put_rows(ref, start, rows):
    base = pl.multiple_of((start >> 3) << 3, 8)
    shift = start - base
    padded = jnp.concatenate([rows, jnp.zeros((8, C), jnp.float32)], axis=0)
    moved = pltpu.roll(padded, shift, 0)
    position = lax.broadcasted_iota(jnp.int32, (8, C), 0)
    pltpu.store(ref.at[pl.ds(base, 8), :], moved[:8], mask=position >= shift)
    ref[pl.ds(pl.multiple_of(base + 8, 8), CELL), :] = moved[8:]


def take_rows(ref, start):
    base = pl.multiple_of((start >> 3) << 3, 8)
    window = ref[pl.ds(base, CELL + 8), :]
    ahead = start - base
    return pltpu.roll(window, jnp.where(ahead == 0, 0, CELL + 8 - ahead), 0)[:CELL]


def table_kernel(rank_ref, count_ref, cell_of, labels, slots, place, label_of, found):
    me = lax.axis_index("cells")
    y, x, z = me >> 4, (me >> 2) & 3, me & 3
    for slot, offset in enumerate(OFFSETS):
        place[number(offset)] = slot
        label_of[slot] = 0
        found[slot] = 0

    def one(cell, carry):
        rank = rank_ref[cell >> 4, cell & 15]
        owner = rank >> 6
        oy = ((owner >> 4) - y) & 3
        ox = (((owner >> 2) & 3) - x) & 3
        oz = ((owner & 3) - z) & 3
        slot = place[(oy << 4) | (ox << 2) | oz]
        slots[cell] = slot
        found[slot] = cell
        label_of[slot] = count_ref[cell >> 4, cell & 15] + 64 * ((rank >> 5) & 1)
        return carry

    lax.fori_loop(0, CELLS_DEV, one, 0)
    for slot in range(SLOTS):
        cell_of[slot] = found[slot]
        labels[slot] = jnp.full((1, 128), label_of[slot], jnp.int32)


def meet(others):
    core = lax.axis_index("patch")
    barrier = pltpu.get_barrier_semaphore()
    for other in others[1:]:
        pl.semaphore_signal(barrier, inc=1, device_id=(core, other), device_id_type=MESH)
    pl.semaphore_signal(
        barrier, inc=1, device_id=(1 - core, lax.axis_index("cells")), device_id_type=MESH
    )
    return barrier


def batch_mlp(batch, arrived, done, gain_row, w_up, w_down):
    slots = pl.ds(pl.multiple_of(batch * BATCH, BATCH), BATCH)
    rows = arrived[slots].reshape(BATCH * CELL, C).astype(jnp.float32)
    rows = mlp_rows(rows, gain_row, w_up, w_down)
    done[slots] = rows.astype(jnp.bfloat16).reshape(BATCH, CELL, C)


def forward_kernel(
    cell_of, labels, features, gains, up_hbm, down_hbm, own, other, own_labels, other_labels,
    send, arrived, arrived_labels, done, w_up, w_down,
    send_sem, recv_sem, label_send, label_recv, keep_sem, pass_sem, got_sem, tail_sem, sems,
):
    core = lax.axis_index("patch")
    sibling = (1 - core, lax.axis_index("cells"))
    others = peers(1)
    barrier = meet(others)
    weights = [
        pltpu.make_async_copy(up_hbm.at[0], w_up, sems.at[0]),
        pltpu.make_async_copy(down_hbm.at[0], w_down, sems.at[1]),
    ]
    for copy in weights:
        copy.start()
    for slot in range(SLOTS):
        send[slot] = features[cell_of[slot]]
    pl.semaphore_wait(barrier, SLOTS)

    pltpu.make_async_copy(send.at[0], arrived.at[0], recv_sem.at[0]).start()
    local_labels = pltpu.make_async_copy(labels.at[0], arrived_labels.at[0], tail_sem.at[3])
    local_labels.start()
    for slot in range(1, SLOTS):
        pltpu.make_async_remote_copy(
            send.at[slot], arrived.at[slot], send_sem, recv_sem.at[slot],
            device_id=(core, others[slot]), device_id_type=MESH,
        ).start()
    for slot in range(1, SLOTS):
        pltpu.make_async_remote_copy(
            labels.at[slot], arrived_labels.at[slot], label_send, label_recv,
            device_id=(core, others[slot]), device_id_type=MESH,
        ).start()
    for copy in weights:
        copy.wait()

    def step(batch, carry):
        for index in range(BATCH):
            slot = batch * BATCH + index
            pltpu.make_async_copy(send.at[slot], arrived.at[slot], recv_sem.at[slot]).wait()
        batch_mlp(batch, arrived, done, gains[0:1, :], w_up, w_down)
        slots = pl.ds(pl.multiple_of(batch * BATCH, BATCH), BATCH)
        pltpu.make_async_copy(done.at[slots], own.at[slots], keep_sem.at[batch]).start()
        pltpu.make_async_remote_copy(
            done.at[slots], other.at[slots], pass_sem.at[batch], got_sem.at[batch],
            device_id=sibling, device_id_type=MESH,
        ).start()
        return carry

    lax.fori_loop(0, BATCHES, step, 0)
    remote = pl.ds(1, SLOTS - 1)
    all_labels = pltpu.make_async_remote_copy(
        labels.at[remote], arrived_labels.at[remote], label_send, label_recv,
        device_id=sibling, device_id_type=MESH,
    )
    all_labels.wait_recv()
    local_labels.wait()
    keep_labels = pltpu.make_async_copy(arrived_labels, own_labels, tail_sem.at[0])
    pass_labels = pltpu.make_async_remote_copy(
        arrived_labels, other_labels, tail_sem.at[1], tail_sem.at[2],
        device_id=sibling, device_id_type=MESH,
    )
    keep_labels.start()
    pass_labels.start()
    all_labels.wait_send()
    pltpu.make_async_remote_copy(
        send.at[remote], arrived.at[remote], send_sem, recv_sem.at[0],
        device_id=sibling, device_id_type=MESH,
    ).wait_send()

    def drain(batch, carry):
        slots = pl.ds(pl.multiple_of(batch * BATCH, BATCH), BATCH)
        pltpu.make_async_copy(done.at[slots], own.at[slots], keep_sem.at[batch]).wait()
        pltpu.make_async_remote_copy(
            done.at[slots], other.at[slots], pass_sem.at[batch], got_sem.at[batch],
            device_id=sibling, device_id_type=MESH,
        ).wait()
        return carry

    lax.fori_loop(0, BATCHES, drain, 0)
    keep_labels.wait()
    pass_labels.wait()


def layer_kernel(
    own_labels, other_labels, own, other, gains, w_qkv, w_out,
    send, packed, queries, keys, values, mixed, ahead, offsets, own_filled, other_filled,
):
    def pack(labels, cells, filled, starts):
        count = jnp.int32(0)
        for slot in range(SLOTS):
            filled[count] = slot
            count = count + jnp.where(labels[slot, 0] > 0, 1, 0)

        def one(cell, starts):
            slot = filled[cell]
            label = labels[slot, 0]
            patch = label >> 6
            count = label & 63
            start = jnp.where(patch == 0, starts[0], starts[1])
            if labels is own_labels:
                offsets[cell] = start
            put_rows(packed.at[patch], start, cells[slot].astype(jnp.float32))
            first = jnp.where(patch == 0, count, 0)
            return starts[0] + first, starts[1] + count - first

        return lax.fori_loop(0, CELLS_DEV, one, starts, unroll=4)

    pack_own = functools.partial(pack, own_labels, own, own_filled)
    pack_other = functools.partial(pack, other_labels, other, other_filled)
    query_rows = pack_own((jnp.int32(0), jnp.int32(0)))
    key_rows = pack_other(query_rows)
    lane = lax.broadcasted_iota(jnp.int32, (1, GROUP_LANES), 1) // DEPTH
    head_masks = [(lane == head).astype(jnp.float32) for head in range(GROUP_HEADS)]

    def project(patch, key_count, step, carry):
        base = pl.multiple_of(step * TM, TM)
        rows = pl.ds(base, TM)
        normed = norm_rows(packed[patch, rows, :], gains[1:2, :])
        raw = jnp.dot(normed, w_qkv[...], preferred_element_type=jnp.float32)
        projected = raw.astype(jnp.bfloat16)
        seen = lax.broadcasted_iota(jnp.int32, (GROUP_LANES, TM), 1) + base < key_count
        ones = lax.broadcasted_iota(jnp.int32, (DEPTH, TM), 1) + base < key_count
        for group in range(GROUPS):
            low = group * GROUP_LANES
            query = raw[:, low : low + GROUP_LANES] * QUERY_SCALE
            queries[group, rows, :] = query.astype(jnp.bfloat16)
            keys[group, rows, :] = projected[:, C + low : C + low + GROUP_LANES]
            value = projected[:, 2 * C + low : 2 * C + low + GROUP_LANES].astype(jnp.float32)
            values[group, :GROUP_LANES, rows] = jnp.where(seen, value.T, 0.0).astype(jnp.bfloat16)
            values[group, GROUP_LANES:, rows] = jnp.where(ones, 1.0, 0.0).astype(jnp.bfloat16)
        return carry

    fold = lax.broadcasted_iota(jnp.int32, (TQ, STACK), 1) % TQ
    fold = fold == lax.broadcasted_iota(jnp.int32, (TQ, STACK), 0)
    fold = fold.astype(jnp.float32).astype(jnp.bfloat16)
    block = lax.broadcasted_iota(jnp.int32, (GROUP_LANES, STACK), 0) // DEPTH
    block = block == lax.broadcasted_iota(jnp.int32, (GROUP_LANES, STACK), 1) // TQ

    def score(group, key_span, tile):
        query = queries[group, pl.ds(pl.multiple_of(tile * TQ, TQ), TQ), :].astype(jnp.float32)
        stacked = jnp.concatenate([query * mask for mask in head_masks], axis=0)
        return lax.dot_general(
            keys[group, :key_span, :], stacked.astype(jnp.bfloat16),
            (((1,), (1,)), ((), ())), preferred_element_type=jnp.float32,
        )

    def weigh(scores):
        highest = jnp.max(scores, axis=0, keepdims=True)
        return jnp.exp2(scores - highest).astype(jnp.bfloat16)

    def mix(group, key_span, weights):
        mixture = jnp.dot(
            values[group, :, :key_span], weights, preferred_element_type=jnp.float32
        )
        top = mixture[:GROUP_LANES] / mixture[GROUP_LANES : GROUP_LANES + 1]
        return jnp.where(block, top, 0.0).astype(jnp.bfloat16)

    def attend(key_span, steps):
        ahead[0, :key_span, :] = score(0, key_span, 0)
        ahead[1, :key_span, :] = score(1, key_span, 0)

        def one(step, carry):
            rows = pl.ds(pl.multiple_of(step * TQ, TQ), TQ)
            following = jnp.minimum(step + 1, steps - 1)
            late = [score(2, key_span, step), score(3, key_span, step)]
            weights = [weigh(ahead[0, :key_span, :]), weigh(ahead[1, :key_span, :])]
            tops = [mix(group, key_span, weights[group]) for group in range(2)]
            early = [score(0, key_span, following), score(1, key_span, following)]
            weights = [weigh(value) for value in late]
            for group in range(2):
                ahead[group, :key_span, :] = early[group]
            tops += [mix(group + 2, key_span, weights[group]) for group in range(2)]
            for group, top in enumerate(tops):
                low = group * GROUP_LANES
                mixed[rows, low : low + GROUP_LANES] = lax.dot_general(
                    fold, top, (((1,), (1,)), ((), ())), preferred_element_type=jnp.float32
                ).astype(jnp.bfloat16)
            return carry

        lax.fori_loop(0, steps, one, 0)

    def finish(patch, step, carry):
        rows = pl.ds(pl.multiple_of(step * TM, TM), TM)
        middle = packed[patch, rows, :] + jnp.dot(
            mixed[rows, :], w_out[...], preferred_element_type=jnp.float32
        )
        packed[patch, rows, :] = middle
        return carry

    def one_patch(patch, carry):
        query_count = jnp.where(patch == 0, query_rows[0], query_rows[1])
        key_count = jnp.where(patch == 0, key_rows[0], key_rows[1])
        base = pl.multiple_of(key_count // 8 * 8, 8)
        spare = jnp.broadcast_to(packed[patch, 0:1, :], (8, C))
        edge = packed[patch, pl.ds(base, 8), :]
        position = lax.broadcasted_iota(jnp.int32, (8, C), 0)
        packed[patch, pl.ds(base, 8), :] = jnp.where(position < key_count - base, edge, spare)
        packed[patch, pl.ds(pl.multiple_of(base + 8, 8), TK), :] = jnp.broadcast_to(spare[:1], (TK, C))
        key_tiles = (key_count + TK - 1) // TK
        lax.fori_loop(0, key_tiles, functools.partial(project, patch, key_count), 0)
        steps = (query_count + TQ - 1) // TQ
        for tiles in range(1, PATCH_ROWS // TK + 1):

            @pl.when(key_tiles == tiles)
            def _():
                attend(tiles * TK, steps)

        lax.fori_loop(0, (query_count + TM - 1) // TM, functools.partial(finish, patch), 0)
        return carry

    lax.fori_loop(0, 2, one_patch, 0)

    def unpack(cell, carry):
        slot = own_filled[cell]
        rows = take_rows(packed.at[own_labels[slot, 0] >> 6], offsets[cell])
        send[slot] = rows.astype(jnp.bfloat16)
        return carry

    lax.fori_loop(0, CELLS_DEV, unpack, 0, unroll=4)


def return_kernel(
    slots, counts, send, gains, up_hbm, down_hbm, out,
    arrived, done, w_up, w_down, send_sem, recv_sem, sems,
):
    core = lax.axis_index("patch")
    others = peers(-1)
    barrier = meet(others)
    weights = [
        pltpu.make_async_copy(up_hbm.at[1], w_up, sems.at[0]),
        pltpu.make_async_copy(down_hbm.at[1], w_down, sems.at[1]),
    ]
    for copy in weights:
        copy.start()
    pl.semaphore_wait(barrier, SLOTS)
    pltpu.make_async_copy(send.at[0], arrived.at[0], recv_sem.at[0]).start()
    for slot in range(1, SLOTS):
        pltpu.make_async_remote_copy(
            send.at[slot], arrived.at[slot], send_sem, recv_sem.at[slot],
            device_id=(core, others[slot]), device_id_type=MESH,
        ).start()
    for copy in weights:
        copy.wait()

    def step(batch, carry):
        for index in range(BATCH):
            slot = batch * BATCH + index
            pltpu.make_async_copy(send.at[slot], arrived.at[slot], recv_sem.at[slot]).wait()
        batch_mlp(batch, arrived, done, gains[2:3, :], w_up, w_down)
        return carry

    lax.fori_loop(0, BATCHES, step, 0)
    remote = pl.ds(1, SLOTS - 1)
    pltpu.make_async_remote_copy(
        send.at[remote], arrived.at[remote], send_sem, recv_sem.at[0],
        device_id=(1 - core, lax.axis_index("cells")), device_id_type=MESH,
    ).wait_send()
    position = lax.broadcasted_iota(jnp.int32, (CELL, C), 0)
    for cell in range(CELLS_DEV):
        rows = done[slots[cell]].astype(jnp.float32)
        count = counts[cell // HALF_CELLS, cell % HALF_CELLS]
        out[cell] = jnp.where(position < count, rows, 0.0).astype(jnp.bfloat16)


def any_spec():
    return pl.BlockSpec(memory_space=pl.ANY)


def hbm_spec():
    return pl.BlockSpec(memory_space=pltpu.HBM)


def vmem_spec():
    return pl.BlockSpec(memory_space=pltpu.VMEM)


def smem_spec():
    return pl.BlockSpec(memory_space=pltpu.SMEM)


def shards(features, hilbert_rank, valid_count, norm_gains, w_qkv, w_out, w_up, w_down):
    slab = jax.ShapeDtypeStruct((SLOTS, CELL, C), jnp.bfloat16)
    label_shape = jax.ShapeDtypeStruct((SLOTS, 1, 128), jnp.int32)
    dma = pltpu.SemaphoreType.DMA
    slab_vmem = pltpu.VMEM((SLOTS, CELL, C), jnp.bfloat16)
    up_vmem = pltpu.VMEM((C, FF), jnp.bfloat16)
    down_vmem = pltpu.VMEM((FF, C), jnp.bfloat16)
    cell_of, labels, slots = pl.pallas_call(
        table_kernel,
        out_shape=(
            jax.ShapeDtypeStruct((SLOTS,), jnp.int32),
            label_shape,
            jax.ShapeDtypeStruct((CELLS_DEV,), jnp.int32),
        ),
        in_specs=[smem_spec(), smem_spec()],
        out_specs=(smem_spec(), vmem_spec(), smem_spec()),
        scratch_shapes=[
            pltpu.SMEM((SLOTS,), jnp.int32),
            pltpu.SMEM((SLOTS,), jnp.int32),
            pltpu.SMEM((SLOTS,), jnp.int32),
        ],
        compiler_params=pltpu.CompilerParams(vmem_limit_bytes=4 * 1024 * 1024),
        cost_estimate=pl.CostEstimate(flops=10**9, bytes_accessed=4 * 10**6, transcendentals=0),
        name="tables",
    )(hilbert_rank, valid_count)

    own, other, own_labels, other_labels = pl.pallas_call(
        forward_kernel,
        out_shape=(slab, slab, label_shape, label_shape),
        in_specs=[smem_spec(), vmem_spec(), vmem_spec(), vmem_spec(), hbm_spec(), hbm_spec()],
        out_specs=(any_spec(), any_spec(), any_spec(), any_spec()),
        scratch_shapes=[
            slab_vmem, slab_vmem, pltpu.VMEM((SLOTS, 1, 128), jnp.int32), slab_vmem,
            up_vmem, down_vmem,
            dma, dma((SLOTS,)), dma, dma,
            dma((BATCHES,)), dma((BATCHES,)), dma((BATCHES,)), dma((4,)), dma((2,)),
        ],
        compiler_params=pltpu.CompilerParams(
            collective_id=0, has_side_effects=True, vmem_limit_bytes=FORWARD_LIMIT
        ),
        cost_estimate=pl.CostEstimate(
            flops=2 * 10**10, bytes_accessed=4 * 10**7, transcendentals=0
        ),
        name="forward",
    )(cell_of, labels, features.reshape(CELLS_DEV, CELL, C), norm_gains, w_up, w_down)

    send = pl.pallas_call(
        layer_kernel,
        out_shape=slab,
        in_specs=[smem_spec(), smem_spec()] + [vmem_spec()] * 5,
        out_specs=vmem_spec(),
        scratch_shapes=[
            pltpu.VMEM((2, PATCH_ROWS + 2 * TK, C), jnp.float32),
            pltpu.VMEM((GROUPS, PATCH_ROWS, GROUP_LANES), jnp.bfloat16),
            pltpu.VMEM((GROUPS, PATCH_ROWS, GROUP_LANES), jnp.bfloat16),
            pltpu.VMEM((GROUPS, GROUP_LANES + DEPTH, PATCH_ROWS), jnp.bfloat16),
            pltpu.VMEM((HALF_ROWS, C), jnp.bfloat16),
            pltpu.VMEM((2, PATCH_ROWS, STACK), jnp.float32),
            pltpu.SMEM((CELLS_DEV,), jnp.int32),
            pltpu.SMEM((SLOTS + 1,), jnp.int32),
            pltpu.SMEM((SLOTS + 1,), jnp.int32),
        ],
        compiler_params=pltpu.CompilerParams(vmem_limit_bytes=LAYER_LIMIT),
        cost_estimate=pl.CostEstimate(
            flops=2 * 10**10, bytes_accessed=4 * 10**7, transcendentals=0
        ),
        name="layer",
    )(
        own_labels.reshape(SLOTS, 128), other_labels.reshape(SLOTS, 128), own, other, norm_gains,
        w_qkv, w_out,
    )

    out = pl.pallas_call(
        return_kernel,
        out_shape=jax.ShapeDtypeStruct((CELLS_DEV, CELL, C), jnp.bfloat16),
        in_specs=[smem_spec(), smem_spec(), any_spec(), vmem_spec(), hbm_spec(), hbm_spec()],
        out_specs=vmem_spec(),
        scratch_shapes=[
            slab_vmem, slab_vmem, up_vmem, down_vmem, dma, dma((SLOTS,)), dma((2,)),
        ],
        compiler_params=pltpu.CompilerParams(
            collective_id=1, has_side_effects=True, vmem_limit_bytes=RETURN_LIMIT
        ),
        cost_estimate=pl.CostEstimate(
            flops=2 * 10**10, bytes_accessed=4 * 10**7, transcendentals=0
        ),
        name="homeward",
    )(slots, valid_count, send, norm_gains, w_up, w_down)
    return out.reshape(features.shape)


def solution(mesh):
    in_specs = (
        P("cells", "patch", None),
        P("cells", "patch"),
        P("cells", "patch"),
        P(),
        P(),
        P(),
        P(),
        P(),
    )
    out_specs = P("cells", "patch", None)
    return jax.shard_map(shards, mesh=mesh, in_specs=in_specs, out_specs=out_specs, check_vma=False)
```

profile of v0, /device:TPU:1, one launch (start us, length us, event | category | flops | bytes accessed | tf_op | source)
XLA Modules:
  0.0 120.2 jit_solution(8223081531959415108)
XLA Ops:
  0.0 0.0 copy-start.5
  0.0 0.0 copy-start.3
  0.0 0.0 copy-start.6
  0.0 0.8 copy-done.6
  0.8 0.0 copy-start.7
  0.8 0.7 copy-done.7
  1.5 2.0 %tables.1 = (s32[64]{0:T(128)S(1)}, s32[64,1,128]{2,1,0:T(1,128)S(1)}, s32[32]{0:T(128)S(1)}) custom-call(s32[2,16]{1,0:T(2,128)S(1)} %copy-done.6, s32[2,16]{1,0:T(2,128)S(1)} %copy-done.7), custom_call_target="tpu_custom_call" | custom-call | flops 1000000000 | bytes 4000000 | tf_op jit(solution)/shard_map/tables/pallas_call | solution.py:427
  3.4 0.0 copy-done.5
  3.4 0.0 copy-done.3
  3.5 0.0 copy-start.2
  3.5 0.0 copy-start.4
  3.5 47.3 %forward.1 = (bf16[64,32,512]{2,1,0:T(8,128)(2,1)S(1)}, bf16[64,32,512]{2,1,0:T(8,128)(2,1)S(1)}, s32[64,1,128]{2,1,0:T(1,128)S(1)}, s32[64,1,128]{2,1,0:T(1,128)S(1)}) custom-call(s32[64]{0:T(128)S(1)} %get-tuple-element.13.cell_of, s32[64,1,128]{2,1,0:T(1,128)S(1)} %get-tuple-element.14.labels, bf16[32,32,512]{2,1,0:T(8,128)(2,1)S(1)} %bitcast.5, ...), custom_call_target="tpu_custom_call" | custom-call | flops 20000000000 | bytes 40000000 | tf_op jit(solution)/shard_map/forward/pallas_call | solution.py:446
  50.8 0.0 copy-done.2
  50.8 0.0 copy-done.4
  50.8 0.0 copy-start
  50.8 0.0 copy-start.1
  50.8 0.0 copy-start.8
  50.8 34.3 %layer.1.send = bf16[64,32,512]{2,1,0:T(8,128)(2,1)S(1)} custom-call(s32[64,128]{1,0:T(8,128)S(1)} %bitcast.6, s32[64,128]{1,0:T(8,128)S(1)} %bitcast.7, bf16[64,32,512]{2,1,0:T(8,128)(2,1)S(1)} %get-tuple-element.17.own, bf16[64,32,512]{2,1,0:T(8,128)(2,1)S(1)} %get-tuple-element.18.other, f32[3,512]{1,0:T(4,128)S(1)} %copy-done.5, ...), custom_call_target="tpu_custom_call" | custom-call | flops 20000000000 | bytes 40000000 | tf_op jit(solution)/shard_map/layer/pallas_call | solution.py:466
  85.2 0.0 copy-done
  85.2 0.0 copy-done.1
  85.2 0.0 copy-done.8
  85.2 34.0 %homeward.1 = bf16[32,32,512]{2,1,0:T(8,128)(2,1)S(1)} custom-call(s32[32]{0:T(128)S(1)} %get-tuple-element.12.slots, s32[2,16]{1,0:T(2,128)S(1)} %copy-done.8, bf16[64,32,512]{2,1,0:T(8,128)(2,1)S(1)} %layer.1.send, f32[3,512]{1,0:T(4,128)S(1)} %copy-done.5, bf16[2,512,2048]{2,1,0:T(8,128)(2,1)S(1)} %copy-done, bf16[2,2048,512]{2,1,0:T(8,128)(2,1)S(1)} %copy-done.1), custom_call_target="tpu_custom_call" | custom-call | flops 20000000000 | bytes 40000000 | tf_op jit(solution)/shard_map/homeward/pallas_call | solution.py:492
  119.2 1.0 copy.10
Async XLA Ops:
  0.0 3.4 %copy-start.5 = (f32[3,512]{1,0:T(4,128)S(1)}, f32[3,512]{1,0:T(4,128)}, u32[]{:S(2)}) copy-start(f32[3,512]{1,0:T(4,128)} %gains.5) | copy-start | bytes 18436
  0.0 3.4 %copy-start.3 = (bf16[2,512,512]{2,1,0:T(8,128)(2,1)S(1)}, bf16[2,512,512]{2,1,0:T(8,128)(2,1)}, u32[]{:S(2)}) copy-start(bf16[2,512,512]{2,1,0:T(8,128)(2,1)} %param.8) | copy-start | bytes 3145732
  0.0 0.8 copy-start.6
  0.8 0.7 copy-start.7
  3.5 47.3 %copy-start.2 = (bf16[512,1536]{1,0:T(8,128)(2,1)S(1)}, bf16[512,1536]{1,0:T(8,128)(2,1)}, u32[]{:S(2)}) copy-start(bf16[512,1536]{1,0:T(8,128)(2,1)} %w_qkv.1) | copy-start | bytes 4718596
  3.5 47.3 %copy-start.4 = (bf16[512,512]{1,0:T(8,128)(2,1)S(1)}, bf16[512,512]{1,0:T(8,128)(2,1)}, u32[]{:S(2)}) copy-start(bf16[512,512]{1,0:T(8,128)(2,1)} %w_out.1) | copy-start | bytes 1572868
  50.8 34.4 %copy-start = (bf16[2,512,2048]{2,1,0:T(8,128)(2,1)S(1)}, bf16[2,512,2048]{2,1,0:T(8,128)(2,1)}, u32[]{:S(2)}) copy-start(bf16[2,512,2048]{2,1,0:T(8,128)(2,1)} %up_hbm.3) | copy-start | bytes 12582916
  50.8 34.4 %copy-start.1 = (bf16[2,2048,512]{2,1,0:T(8,128)(2,1)S(1)}, bf16[2,2048,512]{2,1,0:T(8,128)(2,1)}, u32[]{:S(2)}) copy-start(bf16[2,2048,512]{2,1,0:T(8,128)(2,1)} %down_hbm.3) | copy-start | bytes 12582916
  50.8 34.4 %copy-start.8 = (s32[2,16]{1,0:T(2,128)S(1)}, s32[2,16]{1,0:T(2,128)}, u32[]{:S(2)}) copy-start(s32[2,16]{1,0:T(2,128)} %counts.1) | copy-start | bytes 388
where the time goes:
time: 122 us; the launch traced here: 120 us
  Pallas kernels  118 us (97%)
  local copies, waits for them, and re-layouts  2.46 us (2%)
    pallas_call x1, Pallas kernels, shards(): pl.pallas_call(forward_kernel, out_shape=(slab, slab, label_shape, label_...  47.3 us
    pallas_call x1, Pallas kernels, shards(): pl.pallas_call(layer_kernel, out_shape=slab, in_specs=[smem_spec(), smem_...  34.3 us
    pallas_call x1, Pallas kernels, shards(): pl.pallas_call(return_kernel, out_shape=jax.ShapeDtypeStruct((CELLS_DEV,...  34 us
    unnamed x19, local copies, waits for them, and re-layouts  2.46 us

commit v1 on v0

--- a/solution.py
+++ b/solution.py
@@ -222,7 +222,7 @@
 
 def layer_kernel(
     own_labels, other_labels, own, other, gains, w_qkv, w_out,
-    send, packed, queries, keys, values, mixed, ahead, offsets, own_filled, other_filled,
+    send, packed, queries, keys, values, mixed, ahead, behind, offsets, own_filled, other_filled,
 ):
     def pack(labels, cells, filled, starts):
         count = jnp.int32(0)
@@ -303,9 +303,11 @@
             following = jnp.minimum(step + 1, steps - 1)
             late = [score(2, key_span, step), score(3, key_span, step)]
             weights = [weigh(ahead[0, :key_span, :]), weigh(ahead[1, :key_span, :])]
+            for group in range(2):
+                behind[group, :key_span, :] = late[group]
+            early = [score(0, key_span, following), score(1, key_span, following)]
             tops = [mix(group, key_span, weights[group]) for group in range(2)]
-            early = [score(0, key_span, following), score(1, key_span, following)]
-            weights = [weigh(value) for value in late]
+            weights = [weigh(behind[group, :key_span, :]) for group in range(2)]
             for group in range(2):
                 ahead[group, :key_span, :] = early[group]
             tops += [mix(group + 2, key_span, weights[group]) for group in range(2)]
@@ -475,6 +477,7 @@
             pltpu.VMEM((GROUPS, GROUP_LANES + DEPTH, PATCH_ROWS), jnp.bfloat16),
             pltpu.VMEM((HALF_ROWS, C), jnp.bfloat16),
             pltpu.VMEM((2, PATCH_ROWS, STACK), jnp.float32),
+            pltpu.VMEM((2, PATCH_ROWS, STACK), jnp.float32),
             pltpu.SMEM((CELLS_DEV,), jnp.int32),
             pltpu.SMEM((SLOTS + 1,), jnp.int32),
             pltpu.SMEM((SLOTS + 1,), jnp.int32),

time: 122 us -> 120 us (0.984); the launches traced: 120 us -> 122 us
    pallas_call x1, Pallas kernels: 34 us -> 42.2 us  [shards(): pl.pallas_call(return_kernel, out_shape=jax.ShapeDtypeStruct((CELLS_DEV,...]
    pallas_call x1, Pallas kernels: 34.3 us -> 27.6 us  [shards(): pl.pallas_call(layer_kernel, out_shape=slab, in_specs=[smem_spec(), smem_...]
where the time goes in v1:
time: 120 us; the launch traced here: 122 us
  Pallas kernels  119 us (99%)
  local copies, waits for them, and re-layouts  2.46 us (2%)
    pallas_call x1, Pallas kernels, shards(): pl.pallas_call(forward_kernel, out_shape=(slab, slab, label_shape, label_...  47.3 us
    pallas_call x1, Pallas kernels, shards(): pl.pallas_call(return_kernel, out_shape=jax.ShapeDtypeStruct((CELLS_DEV,...  42.2 us
    pallas_call x1, Pallas kernels, shards(): pl.pallas_call(layer_kernel, out_shape=slab, in_specs=[smem_spec(), smem_...  27.6 us
    unnamed x19, local copies, waits for them, and re-layouts  2.46 us

profile of v1, /device:TPU:1, one launch (start us, length us, event | category | flops | bytes accessed | tf_op | source)
XLA Modules:
  0.0 121.6 jit_solution(13086570271455687422)
XLA Ops:
  0.0 0.0 copy-start.5
  0.0 0.0 copy-start.3
  0.0 0.0 copy-start.6
  0.0 0.8 copy-done.6
  0.8 0.0 copy-start.7
  0.8 0.7 copy-done.7
  1.5 2.0 %tables.1 = (s32[64]{0:T(128)S(1)}, s32[64,1,128]{2,1,0:T(1,128)S(1)}, s32[32]{0:T(128)S(1)}) custom-call(s32[2,16]{1,0:T(2,128)S(1)} %copy-done.6, s32[2,16]{1,0:T(2,128)S(1)} %copy-done.7), custom_call_target="tpu_custom_call" | custom-call | flops 1000000000 | bytes 4000000 | tf_op jit(solution)/shard_map/tables/pallas_call | solution.py:429
  3.4 0.0 copy-done.5
  3.4 0.0 copy-done.3
  3.5 0.0 copy-start.2
  3.5 0.0 copy-start.4
  3.5 47.3 %forward.1 = (bf16[64,32,512]{2,1,0:T(8,128)(2,1)S(1)}, bf16[64,32,512]{2,1,0:T(8,128)(2,1)S(1)}, s32[64,1,128]{2,1,0:T(1,128)S(1)}, s32[64,1,128]{2,1,0:T(1,128)S(1)}) custom-call(s32[64]{0:T(128)S(1)} %get-tuple-element.13.cell_of, s32[64,1,128]{2,1,0:T(1,128)S(1)} %get-tuple-element.14.labels, bf16[32,32,512]{2,1,0:T(8,128)(2,1)S(1)} %bitcast.5, ...), custom_call_target="tpu_custom_call" | custom-call | flops 20000000000 | bytes 40000000 | tf_op jit(solution)/shard_map/forward/pallas_call | solution.py:448
  50.8 0.0 copy-done.2
  50.8 0.0 copy-done.4
  50.8 0.0 copy-start
  50.8 0.0 copy-start.1
  50.8 0.0 copy-start.8
  50.8 27.6 %layer.1.send = bf16[64,32,512]{2,1,0:T(8,128)(2,1)S(1)} custom-call(s32[64,128]{1,0:T(8,128)S(1)} %bitcast.6, s32[64,128]{1,0:T(8,128)S(1)} %bitcast.7, bf16[64,32,512]{2,1,0:T(8,128)(2,1)S(1)} %get-tuple-element.17.own, bf16[64,32,512]{2,1,0:T(8,128)(2,1)S(1)} %get-tuple-element.18.other, f32[3,512]{1,0:T(4,128)S(1)} %copy-done.5, ...), custom_call_target="tpu_custom_call" | custom-call | flops 20000000000 | bytes 40000000 | tf_op jit(solution)/shard_map/layer/pallas_call | solution.py:468
  78.4 0.0 copy-done
  78.4 0.0 copy-done.1
  78.4 0.0 copy-done.8
  78.4 42.2 %homeward.1 = bf16[32,32,512]{2,1,0:T(8,128)(2,1)S(1)} custom-call(s32[32]{0:T(128)S(1)} %get-tuple-element.12.slots, s32[2,16]{1,0:T(2,128)S(1)} %copy-done.8, bf16[64,32,512]{2,1,0:T(8,128)(2,1)S(1)} %layer.1.send, f32[3,512]{1,0:T(4,128)S(1)} %copy-done.5, bf16[2,512,2048]{2,1,0:T(8,128)(2,1)S(1)} %copy-done, bf16[2,2048,512]{2,1,0:T(8,128)(2,1)S(1)} %copy-done.1), custom_call_target="tpu_custom_call" | custom-call | flops 20000000000 | bytes 40000000 | tf_op jit(solution)/shard_map/homeward/pallas_call | solution.py:495
  120.7 1.0 copy.10
Async XLA Ops:
  0.0 3.4 %copy-start.5 = (f32[3,512]{1,0:T(4,128)S(1)}, f32[3,512]{1,0:T(4,128)}, u32[]{:S(2)}) copy-start(f32[3,512]{1,0:T(4,128)} %gains.5) | copy-start | bytes 18436
  0.0 3.4 %copy-start.3 = (bf16[2,512,512]{2,1,0:T(8,128)(2,1)S(1)}, bf16[2,512,512]{2,1,0:T(8,128)(2,1)}, u32[]{:S(2)}) copy-start(bf16[2,512,512]{2,1,0:T(8,128)(2,1)} %param.8) | copy-start | bytes 3145732
  0.0 0.8 copy-start.6
  0.8 0.7 copy-start.7
  3.5 47.3 %copy-start.2 = (bf16[512,1536]{1,0:T(8,128)(2,1)S(1)}, bf16[512,1536]{1,0:T(8,128)(2,1)}, u32[]{:S(2)}) copy-start(bf16[512,1536]{1,0:T(8,128)(2,1)} %w_qkv.1) | copy-start | bytes 4718596
  3.5 47.3 %copy-start.4 = (bf16[512,512]{1,0:T(8,128)(2,1)S(1)}, bf16[512,512]{1,0:T(8,128)(2,1)}, u32[]{:S(2)}) copy-start(bf16[512,512]{1,0:T(8,128)(2,1)} %w_out.1) | copy-start | bytes 1572868
  50.8 27.6 %copy-start = (bf16[2,512,2048]{2,1,0:T(8,128)(2,1)S(1)}, bf16[2,512,2048]{2,1,0:T(8,128)(2,1)}, u32[]{:S(2)}) copy-start(bf16[2,512,2048]{2,1,0:T(8,128)(2,1)} %up_hbm.3) | copy-start | bytes 12582916
  50.8 27.6 %copy-start.1 = (bf16[2,2048,512]{2,1,0:T(8,128)(2,1)S(1)}, bf16[2,2048,512]{2,1,0:T(8,128)(2,1)}, u32[]{:S(2)}) copy-start(bf16[2,2048,512]{2,1,0:T(8,128)(2,1)} %down_hbm.3) | copy-start | bytes 12582916
  50.8 27.6 %copy-start.8 = (s32[2,16]{1,0:T(2,128)S(1)}, s32[2,16]{1,0:T(2,128)}, u32[]{:S(2)}) copy-start(s32[2,16]{1,0:T(2,128)} %counts.1) | copy-start | bytes 388
